TPU v7x, 32 devices: a whole 2x2x4 slice. The times are simulated.
32 devices in a mesh: aux: 4 (over y, x), blk: 8 (over z, core).
Axes of the slice: x: 2, y: 2, z: 4, core: 2. Of those that a mesh axis runs over, the one named last changes fastest.
Arguments:
- integrals: bfloat16 [2048, 64, 1024], P(('aux', 'blk')), may hold values from -0.5 to 0.5
- metric: bfloat16 [2048, 512], P('aux'), may hold values from -1 to 2
- pair_list: int32 [15, 2], replicated, may hold values from 0 to 7, as said below
- aux_mask: int32 [16, 8], P('aux'), may hold values 0 or 1
Outputs:
- band_rows: float32 [8, 128, 640], P('blk', 'aux')
Inputs may be any that keep to these rules, and one draw needn't show every extreme that they name: `pair_list`: every pair (r, r) appears once; the other rows are distinct pairs (r, r + 1) or (r, r + 2) with both blocks below 8; 7 such rows.
All inputs are finite; a program needn't handle non-finite values. No bound on the sum of `aux_mask` on one device may be relied on, other than what follows from the above.
Results may differ from a plain program's by a relative error of at most 0.0015.
Values may be sent and summed in bfloat16 or wider, within the bound.
A program may use at most 128 MiB of HBM per device.

v0:
```python
import functools

import jax
import jax.numpy as jnp
from jax import lax
from jax.experimental import pallas as pl
from jax.experimental.pallas import tpu as pltpu
from jax.sharding import PartitionSpec as P

BS = 128
QB = 128
SPAN = 3
SUB = 8
PAIR = 2
MESH = pl.DeviceIdType.MESH


def tile_kernel(
    peers, domains, blocks, depth, mask_hbm, pairs_hbm, metric_hbm, x_ref, out_ref,
    mask_ref, pairs_ref, metric_ref,
    slab, wide, ordered, fit_rows, fit_cols, piece_out, piece_in, sum_out, sum_in, weights,
    send_sem, recv_sem, own_sem, piece_send, piece_recv, sum_send, sum_recv, load_sem,
):
    me = lax.axis_index("blk")
    domain = lax.axis_index("aux")
    rows = depth // peers
    group = domains * PAIR
    strip = BS // group
    pair_base = (me // PAIR) * PAIR
    place = domain * PAIR + lax.rem(me, PAIR)
    slots = 2 * SPAN - 1

    loads = [
        pltpu.make_async_copy(mask_hbm, mask_ref, load_sem.at[0]),
        pltpu.make_async_copy(pairs_hbm, pairs_ref, load_sem.at[1]),
        pltpu.make_async_copy(metric_hbm, metric_ref, load_sem.at[2]),
    ]
    for load in loads:
        load.start()
    barrier = pltpu.get_barrier_semaphore()

    def member(off):
        other = lax.rem(place + off, group)
        return {"aux": other // PAIR, "blk": pair_base + lax.rem(other, PAIR)}

    def greet(off, carry):
        pl.semaphore_signal(
            barrier, inc=1, device_id={"blk": lax.rem(me + off, peers)}, device_id_type=MESH
        )
        return carry

    lax.fori_loop(1, peers, greet, 0)
    for turn in range(1, domains):
        for core in range(PAIR):
            pl.semaphore_signal(
                barrier,
                inc=1,
                device_id={"aux": lax.rem(domain + turn, domains), "blk": pair_base + core},
                device_id_type=MESH,
            )
    pl.semaphore_wait(barrier, peers - 1 + (domains - 1) * PAIR)

    def source(block, target):
        return x_ref.at[
            :,
            pl.ds(pl.multiple_of(target * SUB, SUB), SUB),
            pl.ds(pl.multiple_of(block * BS, BS), BS),
        ]

    def landing(block, sender):
        return slab.at[block, pl.ds(pl.multiple_of(sender * rows, rows), rows)]

    def outgoing(block, off):
        target = lax.rem(me + off, peers)
        return pltpu.make_async_remote_copy(
            src_ref=source(block, target),
            dst_ref=landing(block, me),
            send_sem=send_sem.at[block, off],
            recv_sem=recv_sem.at[block, off],
            device_id={"blk": target},
            device_id_type=MESH,
        )

    def incoming(block, off):
        sender = lax.rem(me - off + peers, peers)
        return pltpu.make_async_remote_copy(
            src_ref=source(block, me),
            dst_ref=landing(block, sender),
            send_sem=send_sem.at[block, off],
            recv_sem=recv_sem.at[block, off],
            device_id={"blk": sender},
            device_id_type=MESH,
        )

    def own(block):
        return pltpu.make_async_copy(source(block, me), landing(block, me), own_sem.at[block])

    def launch(block, carry):
        def one(off, inner):
            outgoing(block, off).start()
            return inner

        lax.fori_loop(1, peers, one, 0)
        own(block).start()
        return carry

    lax.fori_loop(0, blocks, launch, 0)

    for load in loads:
        load.wait()
    for slot in range(slots):
        gap = abs(slot - (SPAN - 1))
        row = me if slot >= SPAN - 1 else me - gap
        count = jnp.int32(0)
        for index in range(pairs_ref.shape[1]):
            first = pairs_ref[0, index]
            hit = (first == row) & (pairs_ref[1, index] - first == gap)
            count = count + hit.astype(jnp.int32)
        weights[slot] = count.astype(jnp.float32)

    fit_cols[: (SPAN - 1) * BS, :] = jnp.zeros(((SPAN - 1) * BS, SUB * depth), jnp.bfloat16)
    for gap in range(1, SPAN):

        @pl.when(me + gap >= blocks)
        def _():
            sum_in[:, SPAN - 1 + gap] = jnp.zeros((peers, strip, BS), jnp.float32)

    def piece_to(block, off):
        return pltpu.make_async_remote_copy(
            src_ref=piece_out.at[block, lax.rem(place + off, group)],
            dst_ref=piece_in.at[block, place],
            send_sem=piece_send.at[block, off],
            recv_sem=piece_recv.at[block, off],
            device_id=member(off),
            device_id_type=MESH,
        )

    def piece_from(block, off):
        sender = lax.rem(place - off + group, group)
        return pltpu.make_async_remote_copy(
            src_ref=piece_out.at[block, sender],
            dst_ref=piece_in.at[block, sender],
            send_sem=piece_send.at[block, off],
            recv_sem=piece_recv.at[block, off],
            device_id=member(group - off),
            device_id_type=MESH,
        )

    def span_of(gap):
        return pl.ds(0, SPAN) if gap == 0 else pl.ds(SPAN - 1 + gap, 1)

    def sum_to(block, gap):
        return pltpu.make_async_remote_copy(
            src_ref=sum_out.at[block, span_of(gap)],
            dst_ref=sum_in.at[me, span_of(gap)],
            send_sem=sum_send.at[block, gap],
            recv_sem=sum_recv.at[me, gap],
            device_id={"blk": block - gap},
            device_id_type=MESH,
        )

    def sum_from(sender, gap):
        return pltpu.make_async_remote_copy(
            src_ref=sum_out.at[0, span_of(gap)],
            dst_ref=sum_in.at[sender, span_of(gap)],
            send_sem=sum_send.at[0, gap],
            recv_sem=sum_recv.at[sender, gap],
            device_id={"blk": sender},
            device_id_type=MESH,
        )

    def pass_on(block):
        def arrive(off, inner):
            piece_from(block, off).wait_recv()
            return inner

        lax.fori_loop(1, group, arrive, 0)
        total = piece_out[block, place]
        for off in range(1, group):
            total = total + piece_in[block, lax.rem(place + off, group)]
        sum_out[block] = total
        for gap in range(SPAN):
            owner = block - gap

            @pl.when(owner == me)
            def _():
                if gap == 0:
                    sum_in[me, :SPAN] = total[:SPAN]
                else:
                    sum_in[me, SPAN - 1 + gap] = total[SPAN - 1 + gap]

    def ship(block, carry):
        for gap in range(SPAN):
            owner = block - gap

            @pl.when((owner >= 0) & (owner != me))
            def _():
                sum_to(block, gap).start()

        return carry

    def reorder(block, sender):
        span = pl.ds(pl.multiple_of(sender * rows, rows), rows)
        wide[...] = slab[block, span].reshape(rows * SUB, BS).astype(jnp.float32)
        for i in range(SUB):
            ordered[span, i * BS : (i + 1) * BS] = wide[pl.ds(i, rows, stride=SUB), :].astype(
                jnp.bfloat16
            )

    def step(block, carry):
        @pl.when(block > 0)
        def _():
            pass_on(block - 1)

        def arrive(off, inner):
            incoming(block, off).wait_recv()
            reorder(block, lax.rem(me - off + peers, peers))
            return inner

        own(block).wait()
        reorder(block, me)
        lax.fori_loop(1, peers, arrive, 0)

        @pl.when(block == blocks - 1)
        def _():
            lax.fori_loop(0, blocks - 1, ship, 0)

        for qb in range(depth // QB):
            keep = mask_ref[qb, block].astype(jnp.float32)
            fitted = jnp.dot(
                metric_ref[qb * QB : (qb + 1) * QB, :],
                ordered[...],
                preferred_element_type=jnp.float32,
            )
            fitted = (fitted * keep).astype(jnp.bfloat16)
            for i in range(SUB):
                piece = fitted[:, i * BS : (i + 1) * BS]
                at = i * depth + qb * QB
                fit_rows[at : at + QB, :] = piece
                fit_cols[
                    pl.ds(pl.multiple_of((block + SPAN - 1) * BS, BS), BS), at : at + QB
                ] = piece.T
        tiles = jnp.dot(
            fit_cols[pl.ds(pl.multiple_of(block * BS, BS), SPAN * BS), :],
            fit_rows[...],
            preferred_element_type=jnp.float32,
        )
        for gap in range(SPAN):
            at = (SPAN - 1 - gap) * BS
            tile = tiles[at : at + BS, :]
            piece_out[block, :, SPAN - 1 + gap] = tile.reshape(group, strip, BS)
            if gap > 0:
                piece_out[block, :, SPAN - 1 - gap] = tile.T.reshape(group, strip, BS)

        def one(off, inner):
            piece_to(block, off).start()
            return inner

        lax.fori_loop(1, group, one, 0)
        return carry

    lax.fori_loop(0, blocks, step, 0)
    pass_on(blocks - 1)
    ship(blocks - 1, 0)

    for gap in range(SPAN):

        @pl.when(me + gap < blocks)
        def _():
            def arrive(off, inner):
                sum_from(lax.rem(me + off, peers), gap).wait_recv()
                return inner

            lax.fori_loop(1, peers, arrive, 0)

    for core in range(PAIR):
        for slot in range(slots):
            total = sum_in[core, slot]
            for turn in range(1, peers // PAIR):
                total = total + sum_in[turn * PAIR + core, slot]
            out_ref[0, core * strip : (core + 1) * strip, slot * BS : (slot + 1) * BS] = (
                total * weights[slot]
            )

    def settle(block, carry):
        def one(off, inner):
            outgoing(block, off).wait_send()
            return inner

        def two(off, inner):
            piece_to(block, off).wait_send()
            return inner

        lax.fori_loop(1, peers, one, 0)
        lax.fori_loop(1, group, two, 0)
        for gap in range(SPAN):
            owner = block - gap

            @pl.when((owner >= 0) & (owner != me))
            def _():
                sum_to(block, gap).wait_send()

        return carry

    lax.fori_loop(0, blocks, settle, 0)


def in_hbm(operand):
    return pltpu.with_memory_space_constraint(operand, pltpu.MemorySpace.HBM)


def by_orbital(integrals, metric, pair_list, aux_mask):
    peers = lax.axis_size("blk")
    domains = lax.axis_size("aux")
    depth = metric.shape[1]
    blocks = aux_mask.shape[1]
    group = domains * PAIR
    slots = 2 * SPAN - 1
    strip = BS // group
    return pl.pallas_call(
        functools.partial(tile_kernel, peers, domains, blocks, depth),
        out_shape=jax.ShapeDtypeStruct((1, BS // domains, slots * BS), jnp.float32),
        in_specs=[
            pl.BlockSpec(memory_space=pl.ANY),
            pl.BlockSpec(memory_space=pl.ANY),
            pl.BlockSpec(memory_space=pl.ANY),
            pl.BlockSpec(memory_space=pl.ANY),
        ],
        out_specs=pl.BlockSpec(memory_space=pltpu.VMEM),
        scratch_shapes=[
            pltpu.SMEM(aux_mask.shape, jnp.int32),
            pltpu.SMEM(pair_list.shape[::-1], jnp.int32),
            pltpu.VMEM(metric.shape, jnp.bfloat16),
            pltpu.VMEM((blocks, depth, SUB, BS), jnp.bfloat16),
            pltpu.VMEM((depth // peers * SUB, BS), jnp.float32),
            pltpu.VMEM((depth, SUB * BS), jnp.bfloat16),
            pltpu.VMEM((SUB * depth, BS), jnp.bfloat16),
            pltpu.VMEM(((blocks + SPAN - 1) * BS, SUB * depth), jnp.bfloat16),
            pltpu.VMEM((blocks, group, slots, strip, BS), jnp.float32),
            pltpu.VMEM((blocks, group, slots, strip, BS), jnp.float32),
            pltpu.VMEM((blocks, slots, strip, BS), jnp.float32),
            pltpu.VMEM((peers, slots, strip, BS), jnp.float32),
            pltpu.SMEM((slots,), jnp.float32),
            pltpu.SemaphoreType.DMA((blocks, peers)),
            pltpu.SemaphoreType.DMA((blocks, peers)),
            pltpu.SemaphoreType.DMA((blocks,)),
            pltpu.SemaphoreType.DMA((blocks, group)),
            pltpu.SemaphoreType.DMA((blocks, group)),
            pltpu.SemaphoreType.DMA((blocks, SPAN)),
            pltpu.SemaphoreType.DMA((peers, SPAN)),
            pltpu.SemaphoreType.DMA((3,)),
        ],
        compiler_params=pltpu.CompilerParams(
            collective_id=0, has_side_effects=True, vmem_limit_bytes=36 * 1024 * 1024
        ),
    )(*[in_hbm(operand) for operand in (aux_mask, pair_list.T, metric, integrals)])


def from_behind(array, axis, by):
    peers = lax.axis_size(axis)
    pairs = [(i, i + by) for i in range(peers) if 0 <= i + by < peers]
    return lax.ppermute(array, axis, pairs)


def fit_block(metric, slab_piece, mask_rows):
    fitted = jnp.einsum("pq,qjn->pjn", metric, slab_piece, preferred_element_type=jnp.float32)
    return (fitted * mask_rows[:, None, None]).astype(jnp.bfloat16)


def by_block(integrals, metric, pair_list, aux_mask):
    block_count = aux_mask.shape[1]
    position = lax.axis_index("blk")
    block_ids = jnp.arange(block_count, dtype=jnp.int32)
    offsets = jnp.arange(SPAN, dtype=jnp.int32)
    col_gap = pair_list[:, 1] - pair_list[:, 0]
    hits = (pair_list[:, 0][:, None] == position) & (col_gap[:, None] == offsets[None, :])
    listed = jnp.sum(hits.astype(jnp.int32), axis=0)
    one_hot = (block_ids == position).astype(jnp.int32)
    column = jnp.sum(aux_mask * one_hot[None, :], axis=1)
    own_mask = jnp.repeat(column, QB).astype(jnp.float32)
    own_block = fit_block(
        metric, lax.all_to_all(integrals, "blk", split_axis=2, concat_axis=0, tiled=True), own_mask
    )
    partners = [own_block]
    current = own_block
    for turn_index in range(SPAN - 1):
        current = from_behind(current, "blk", -1)
        partners.append(current)
    flat_own = partners[0].reshape(-1, BS)

    def make_tile(partner):
        return lax.dot_general(
            flat_own,
            partner.reshape(-1, BS),
            (((0,), (0,)), ((), ())),
            preferred_element_type=jnp.float32,
        )

    tile_list = [
        make_tile(partners[offset]) * listed[offset].astype(jnp.float32) for offset in range(SPAN)
    ]
    upper_tiles = jnp.stack(tile_list)
    mirror_tiles = jnp.stack([jnp.transpose(tile_list[offset]) for offset in range(1, SPAN)])
    lower_tiles = []
    moving = mirror_tiles
    for turn_index in range(SPAN - 1):
        moving = from_behind(moving.astype(jnp.bfloat16), "blk", 1).astype(moving.dtype)
        lower_tiles.append(moving[0])
        moving = moving[1:]
    whole_band = jnp.concatenate(
        [jnp.stack([lower_tiles[SPAN - 2 - slot] for slot in range(SPAN - 1)]), upper_tiles], axis=0
    )
    band_parts = lax.psum_scatter(whole_band, "aux", scatter_dimension=1, tiled=True)
    pieces = [band_parts[slot] for slot in range(2 * SPAN - 1)]
    band_rows = jnp.concatenate(pieces, axis=1)
    return band_rows[None]


def local(integrals, metric, pair_list, aux_mask):
    peers = lax.axis_size("blk")
    blocks = aux_mask.shape[1]
    strips = BS % (8 * PAIR * lax.axis_size("aux")) == 0 and peers % PAIR == 0
    whole_tiles = integrals.shape[1] == SUB * peers and blocks == peers and strips
    if whole_tiles:
        return by_orbital(integrals, metric, pair_list, aux_mask)
    return by_block(integrals, metric, pair_list, aux_mask)


def solution(mesh):
    return jax.shard_map(
        local,
        mesh=mesh,
        in_specs=(P(("aux", "blk"), None, None), P("aux", None), P(), P("aux", None)),
        out_specs=P("blk", "aux", None),
        check_vma=False,
    )
```

profile of v0, /device:TPU:0, one launch (start us, length us, event | category | flops | bytes accessed | tf_op | source)
XLA Modules:
  0.0 197.8 jit_solution(15017203077240436173)
XLA Ops:
  0.0 197.1 %shard_map.46 = f32[1,32,640]{2,1,0:T(8,128)S(1)} custom-call(s32[4,8]{1,0:T(4,128)} %mask_hbm.1, s32[2,15]{1,0:T(2,128)} %bitcast.1, bf16[512,512]{1,0:T(8,128)(2,1)} %metric_hbm.1, bf16[64,64,1024]{2,1,0:T(8,128)(2,1)} %x_ref.1), custom_call_target="tpu_custom_call" | custom-call | tf_op jit(solution)/shard_map/pallas_call | solution.py:320
  197.1 0.6 copy.6
where the time goes:
time: 200 us; the launch traced here: 198 us
  Pallas kernels  197 us (98%)
    pallas_call x1, Pallas kernels, by_orbital(): pl.pallas_call(functools.partial(tile_kernel, peers, domains, blocks, dep...  197 us

commit v1 on v0

v1 whole, which is shorter than its diff:
```python
import functools

import jax
import jax.numpy as jnp
from jax import lax
from jax.experimental import pallas as pl
from jax.experimental.pallas import tpu as pltpu
from jax.sharding import PartitionSpec as P

BS = 128
QB = 128
SPAN = 3
SUB = 8
PAIR = 2
MESH = pl.DeviceIdType.MESH


def tile_kernel(
    peers, domains, blocks, depth, mask_hbm, pairs_hbm, metric_hbm, x_ref, out_ref,
    mask_ref, pairs_ref, metric_ref,
    slab, wide, ordered, fit_rows, fit_cols, piece_out, piece_in, sum_out, sum_in, relay_in,
    tail_out, tail_in, weights,
    send_sem, recv_sem, own_sem, piece_send, piece_recv, sum_send, sum_recv, relay_send,
    relay_recv, tail_send, tail_recv, load_sem,
):
    me = lax.axis_index("blk")
    domain = lax.axis_index("aux")
    rows = depth // peers
    half = peers // 2
    last = blocks - 1
    group = domains * PAIR
    strip = BS // group
    pair_base = (me // PAIR) * PAIR
    place = domain * PAIR + lax.rem(me, PAIR)
    slots = 2 * SPAN - 1
    side = me // half

    def mirror(index, which):
        return index + which * (peers - 1 - 2 * index)

    rank = mirror(me, side)
    outer = rank < PAIR
    is_tail = rank == 0
    sign = 2 * side - 1

    def block_at(step, which):
        return mirror(step, 1 - which)

    loads = [
        pltpu.make_async_copy(mask_hbm, mask_ref, load_sem.at[0]),
        pltpu.make_async_copy(pairs_hbm, pairs_ref, load_sem.at[1]),
        pltpu.make_async_copy(metric_hbm, metric_ref, load_sem.at[2]),
    ]
    for load in loads:
        load.start()
    barrier = pltpu.get_barrier_semaphore()

    def member(off):
        other = lax.rem(place + off, group)
        return {"aux": other // PAIR, "blk": pair_base + lax.rem(other, PAIR)}

    def greet(off, carry):
        pl.semaphore_signal(
            barrier, inc=1, device_id={"blk": lax.rem(me + off, peers)}, device_id_type=MESH
        )
        return carry

    lax.fori_loop(1, peers, greet, 0)
    for turn in range(1, domains):
        for near in range(half):
            pl.semaphore_signal(
                barrier,
                inc=1,
                device_id={"aux": lax.rem(domain + turn, domains), "blk": side * half + near},
                device_id_type=MESH,
            )
    pl.semaphore_wait(barrier, peers - 1 + (domains - 1) * half)

    def source(block, target):
        return x_ref.at[
            :,
            pl.ds(pl.multiple_of(target * SUB, SUB), SUB),
            pl.ds(pl.multiple_of(block * BS, BS), BS),
        ]

    def landing(step, sender):
        return slab.at[step, pl.ds(pl.multiple_of(sender * rows, rows), rows)]

    def outgoing(step, target):
        return pltpu.make_async_remote_copy(
            src_ref=source(block_at(step, target // half), target),
            dst_ref=landing(step, me),
            send_sem=send_sem.at[step, target],
            recv_sem=recv_sem.at[step, me],
            device_id={"blk": target},
            device_id_type=MESH,
        )

    def incoming(step, sender):
        return pltpu.make_async_remote_copy(
            src_ref=source(block_at(step, side), me),
            dst_ref=landing(step, sender),
            send_sem=send_sem.at[step, sender],
            recv_sem=recv_sem.at[step, sender],
            device_id={"blk": sender},
            device_id_type=MESH,
        )

    def own(step):
        return pltpu.make_async_copy(
            source(block_at(step, side), me), landing(step, me), own_sem.at[step]
        )

    def beside(off):
        return side * half + lax.rem(me + off, half)

    def across(other_rank):
        return mirror(other_rank, 1 - side)

    def launch(step, carry):
        for other_rank in range(half - 1, 0, -1):
            outgoing(step, across(other_rank)).start()

        @pl.when(step < last - 1)
        def _():
            outgoing(step, across(0)).start()

        for off in range(1, half):
            outgoing(step, beside(off)).start()
        own(step).start()
        return carry

    lax.fori_loop(0, blocks, launch, 0)
    for step in (last - 1, last):
        outgoing(step, across(0)).start()

    for load in loads:
        load.wait()
    for slot in range(slots):
        gap = abs(slot - (SPAN - 1))
        behind = jnp.minimum(sign * (slot - (SPAN - 1)), 0)
        count = jnp.int32(0)
        for index in range(pairs_ref.shape[1]):
            first = pairs_ref[0, index]
            hit = (first == me + behind) & (pairs_ref[1, index] - first == gap)
            count = count + hit.astype(jnp.int32)
        weights[slot] = count.astype(jnp.float32)

    fit_cols[: (SPAN - 1) * BS, :] = jnp.zeros(((SPAN - 1) * BS, SUB * depth), jnp.bfloat16)
    for gap in range(1, SPAN):

        @pl.when(rank < gap)
        def _():
            sum_in[pl.ds(side * half, half), SPAN - 1 + gap] = jnp.zeros(
                (half, strip, BS), jnp.float32
            )

    def piece_to(step, off):
        return pltpu.make_async_remote_copy(
            src_ref=piece_out.at[step, lax.rem(place + off, group)],
            dst_ref=piece_in.at[step, place],
            send_sem=piece_send.at[step, off],
            recv_sem=piece_recv.at[step, off],
            device_id=member(off),
            device_id_type=MESH,
        )

    def piece_from(step, off):
        sender = lax.rem(place - off + group, group)
        return pltpu.make_async_remote_copy(
            src_ref=piece_out.at[step, sender],
            dst_ref=piece_in.at[step, sender],
            send_sem=piece_send.at[step, off],
            recv_sem=piece_recv.at[step, off],
            device_id=member(group - off),
            device_id_type=MESH,
        )

    def span_of(gap):
        return pl.ds(0, SPAN) if gap == 0 else pl.ds(SPAN - 1 + gap, 1)

    def sum_to(step, gap):
        return pltpu.make_async_remote_copy(
            src_ref=sum_out.at[step, span_of(gap)],
            dst_ref=sum_in.at[me, span_of(gap)],
            send_sem=sum_send.at[step, gap],
            recv_sem=sum_recv.at[me, gap],
            device_id={"blk": block_at(step - gap, side)},
            device_id_type=MESH,
        )

    def sum_from(sender, gap):
        return pltpu.make_async_remote_copy(
            src_ref=sum_out.at[0, span_of(gap)],
            dst_ref=sum_in.at[sender, span_of(gap)],
            send_sem=sum_send.at[0, gap],
            recv_sem=sum_recv.at[sender, gap],
            device_id={"blk": sender},
            device_id_type=MESH,
        )

    def relay(step, gap, other_rank):
        return pltpu.make_async_remote_copy(
            src_ref=sum_out.at[step, span_of(gap)],
            dst_ref=relay_in.at[step, span_of(gap)],
            send_sem=relay_send.at[step, gap],
            recv_sem=relay_recv.at[step, gap],
            device_id={"blk": mirror(other_rank, side)},
            device_id_type=MESH,
        )

    def crossing(step, gap):
        return (step >= gap) & (step - gap < half)

    def staying(step, gap):
        return step - gap >= half

    def gather(step):
        late = outer & (step >= last - 1)

        def arrive(off, inner):
            sender = lax.rem(place - off + group, group)

            @pl.when(jnp.logical_not(late & (lax.rem(sender, PAIR) == side)))
            def _():
                piece_from(step, off).wait_recv()

            return inner

        lax.fori_loop(1, group, arrive, 0)

        @pl.when(late)
        def _():
            total = piece_in[step, 1 - side]
            for turn in range(1, domains):
                total = total + piece_in[step, turn * PAIR + 1 - side]
            sum_out[step] = total

        @pl.when(jnp.logical_not(late))
        def _():
            total = piece_in[step, 0]
            for other in range(1, group):
                total = total + piece_in[step, other]
            sum_out[step] = total

        for gap in range(SPAN):
            owner = block_at(step - gap, side)

            @pl.when(staying(step, gap) & (owner == me))
            def _():
                if gap == 0:
                    sum_in[me, :SPAN] = sum_out[step, :SPAN]
                else:
                    sum_in[me, SPAN - 1 + gap] = sum_out[step, SPAN - 1 + gap]

            @pl.when(staying(step, gap) & (owner != me))
            def _():
                sum_to(step, gap).start()

            @pl.when(crossing(step, gap) & outer)
            def _():
                relay(step, gap, rank + PAIR).start()

    def forward(step):
        for gap in range(SPAN):

            @pl.when(crossing(step, gap) & jnp.logical_not(outer))
            def _():
                relay(step, gap, rank - PAIR).wait_recv()
                if gap == 0:
                    sum_out[step, :SPAN] = sum_out[step, :SPAN] + relay_in[step, :SPAN]
                else:
                    at = SPAN - 1 + gap
                    sum_out[step, at] = sum_out[step, at] + relay_in[step, at]
                sum_to(step, gap).start()

    def reorder(step, sender):
        span = pl.ds(pl.multiple_of(sender * rows, rows), rows)
        wide[...] = slab[step, span].reshape(rows * SUB, BS).astype(jnp.float32)
        for i in range(SUB):
            ordered[span, i * BS : (i + 1) * BS] = wide[pl.ds(i, rows, stride=SUB), :].astype(
                jnp.bfloat16
            )

    def collect(step):
        own(step).wait()
        reorder(step, me)

        def arrive_beside(off, inner):
            incoming(step, beside(off)).wait_recv()
            reorder(step, beside(off))
            return inner

        def arrive_across(other_rank, inner):
            incoming(step, across(other_rank)).wait_recv()
            reorder(step, across(other_rank))
            return inner

        lax.fori_loop(1, half, arrive_beside, 0)
        lax.fori_loop(0, half, arrive_across, 0)

    def multiply(step):
        block = block_at(step, side)
        for qb in range(depth // QB):
            keep = mask_ref[qb, block].astype(jnp.float32)
            fitted = jnp.dot(
                metric_ref[qb * QB : (qb + 1) * QB, :],
                ordered[...],
                preferred_element_type=jnp.float32,
            )
            fitted = (fitted * keep).astype(jnp.bfloat16)
            for i in range(SUB):
                piece = fitted[:, i * BS : (i + 1) * BS]
                at = i * depth + qb * QB
                fit_rows[at : at + QB, :] = piece
                fit_cols[
                    pl.ds(pl.multiple_of((step + SPAN - 1) * BS, BS), BS), at : at + QB
                ] = piece.T
        return jnp.dot(
            fit_cols[pl.ds(pl.multiple_of(step * BS, BS), SPAN * BS), :],
            fit_rows[...],
            preferred_element_type=jnp.float32,
        )

    def pieces(step, tiles):
        for gap in range(SPAN):
            at = (SPAN - 1 - gap) * BS
            tile = tiles[at : at + BS, :]
            piece_out[step, :, SPAN - 1 + gap] = tile.reshape(group, strip, BS)
            if gap > 0:
                piece_out[step, :, SPAN - 1 - gap] = tile.T.reshape(group, strip, BS)
        piece_in[step, place] = piece_out[step, place]

        def one(off, inner):
            piece_to(step, off).start()
            return inner

        lax.fori_loop(1, group, one, 0)

    def tail_to(turn_step, gap, turn):
        to = lax.rem(domain + turn, domains)
        return pltpu.make_async_remote_copy(
            src_ref=tail_out.at[turn_step, to, span_of(gap)],
            dst_ref=tail_in.at[turn_step, domain, span_of(gap)],
            send_sem=tail_send.at[turn_step, gap, turn],
            recv_sem=tail_recv.at[turn_step, gap, domain],
            device_id={"aux": to, "blk": mirror(1 - turn_step + gap, side)},
            device_id_type=MESH,
        )

    def tail_from(turn_step, gap, sender):
        return pltpu.make_async_remote_copy(
            src_ref=tail_out.at[turn_step, sender, span_of(gap)],
            dst_ref=tail_in.at[turn_step, sender, span_of(gap)],
            send_sem=tail_send.at[turn_step, gap, 0],
            recv_sem=tail_recv.at[turn_step, gap, sender],
            device_id={"aux": sender, "blk": mirror(0, side)},
            device_id_type=MESH,
        )

    def tail_sends():
        for turn_step in range(2):
            for gap in range(SPAN):
                for turn in range(domains):
                    if turn > 0 or turn_step == 0 or gap > 0:
                        yield turn_step, gap, turn

    def direct(turn_step, tiles):
        for gap in range(SPAN):
            at = (SPAN - 1 - gap) * BS
            tile = tiles[at : at + BS, :]
            low = (domains, BS // domains, BS)
            tail_out[turn_step, :, SPAN - 1 + gap] = tile.reshape(low).astype(jnp.bfloat16)
            if gap > 0:
                tail_out[turn_step, :, SPAN - 1 - gap] = tile.T.reshape(low).astype(jnp.bfloat16)
        for which, gap, turn in tail_sends():
            if which == turn_step:
                tail_to(turn_step, gap, turn).start()
        if turn_step == 1:
            tail_in[1, domain, :SPAN] = tail_out[1, domain, :SPAN]

    def step(index, carry):
        @pl.when(index > 0)
        def _():
            gather(index - 1)

        @pl.when(index > 1)
        def _():
            forward(index - 2)

        @pl.when(is_tail & (index == last))
        def _():
            gather(last)

        collect(index)
        tiles = multiply(index)
        late = is_tail & (index >= last - 1)

        @pl.when(jnp.logical_not(late))
        def _():
            pieces(index, tiles)

        for turn_step in range(2):

            @pl.when(is_tail & (index == last - 1 + turn_step))
            def _():
                direct(turn_step, tiles)

        return carry

    lax.fori_loop(0, blocks, step, 0)

    @pl.when(jnp.logical_not(is_tail))
    def _():
        gather(last)

    def settle(index, carry):
        for other_rank in range(half):
            outgoing(index, across(other_rank)).wait_send()
        for off in range(1, half):
            outgoing(index, beside(off)).wait_send()

        def two(off, inner):
            piece_to(index, off).wait_send()
            return inner

        @pl.when(jnp.logical_not(is_tail & (index >= last - 1)))
        def _():
            lax.fori_loop(1, group, two, 0)

        for gap in range(SPAN):
            owner = block_at(index - gap, side)
            kept = staying(index, gap) & (owner != me)
            crossed = crossing(index, gap)

            @pl.when(kept | (crossed & jnp.logical_not(outer)))
            def _():
                sum_to(index, gap).wait_send()

            @pl.when(crossed & outer)
            def _():
                relay(index, gap, rank + PAIR).wait_send()

        return carry

    lax.fori_loop(0, blocks, settle, 0)

    inner_base = half - PAIR + (1 - side) * PAIR
    for gap in range(SPAN):

        @pl.when(rank >= gap)
        def _():
            def arrive(off, inner):
                sum_from(beside(off), gap).wait_recv()
                return inner

            lax.fori_loop(1, half, arrive, 0)

        for core in range(PAIR):
            sum_from(inner_base + core, gap).wait_recv()

    for turn_step in range(2):
        for gap in range(SPAN):

            @pl.when(rank == 1 - turn_step + gap)
            def _():
                for sender in range(domains):

                    @pl.when(jnp.logical_not(is_tail & (sender == domain)))
                    def _():
                        tail_from(turn_step, gap, sender).wait_recv()

    for slot in range(slots):
        where = SPAN - 1 + sign * (slot - (SPAN - 1))
        columns = pl.ds(pl.multiple_of(where * BS, BS), BS)
        for core in range(PAIR):
            total = sum_in[inner_base + core, slots - 1 - slot]
            for turn in range(half // PAIR):
                total = total + sum_in[side * half + turn * PAIR + core, slot]
            out_ref[0, core * strip : (core + 1) * strip, columns] = total * weights[slot]

    for turn_step in range(2):
        for gap in range(SPAN):

            @pl.when(rank == 1 - turn_step + gap)
            def _():
                for slot in range(SPAN) if gap == 0 else [SPAN - 1 + gap]:
                    where = SPAN - 1 + sign * (slot - (SPAN - 1))
                    columns = pl.ds(pl.multiple_of(where * BS, BS), BS)
                    total = tail_in[turn_step, 0, slot].astype(jnp.float32)
                    for sender in range(1, domains):
                        total = total + tail_in[turn_step, sender, slot].astype(jnp.float32)
                    out_ref[0, :, columns] = out_ref[0, :, columns] + total * weights[slot]

    for which, gap, turn in tail_sends():

        @pl.when(is_tail)
        def _():
            tail_to(which, gap, turn).wait_send()


def in_hbm(operand):
    return pltpu.with_memory_space_constraint(operand, pltpu.MemorySpace.HBM)


def by_orbital(integrals, metric, pair_list, aux_mask):
    peers = lax.axis_size("blk")
    domains = lax.axis_size("aux")
    depth = metric.shape[1]
    blocks = aux_mask.shape[1]
    group = domains * PAIR
    slots = 2 * SPAN - 1
    strip = BS // group
    return pl.pallas_call(
        functools.partial(tile_kernel, peers, domains, blocks, depth),
        out_shape=jax.ShapeDtypeStruct((1, BS // domains, slots * BS), jnp.float32),
        in_specs=[
            pl.BlockSpec(memory_space=pl.ANY),
            pl.BlockSpec(memory_space=pl.ANY),
            pl.BlockSpec(memory_space=pl.ANY),
            pl.BlockSpec(memory_space=pl.ANY),
        ],
        out_specs=pl.BlockSpec(memory_space=pltpu.VMEM),
        scratch_shapes=[
            pltpu.SMEM(aux_mask.shape, jnp.int32),
            pltpu.SMEM(pair_list.shape[::-1], jnp.int32),
            pltpu.VMEM(metric.shape, jnp.bfloat16),
            pltpu.VMEM((blocks, depth, SUB, BS), jnp.bfloat16),
            pltpu.VMEM((depth // peers * SUB, BS), jnp.float32),
            pltpu.VMEM((depth, SUB * BS), jnp.bfloat16),
            pltpu.VMEM((SUB * depth, BS), jnp.bfloat16),
            pltpu.VMEM(((blocks + SPAN - 1) * BS, SUB * depth), jnp.bfloat16),
            pltpu.VMEM((blocks, group, slots, strip, BS), jnp.float32),
            pltpu.VMEM((blocks, group, slots, strip, BS), jnp.float32),
            pltpu.VMEM((blocks, slots, strip, BS), jnp.float32),
            pltpu.VMEM((peers, slots, strip, BS), jnp.float32),
            pltpu.VMEM((blocks, slots, strip, BS), jnp.float32),
            pltpu.VMEM((2, domains, slots, BS // domains, BS), jnp.bfloat16),
            pltpu.VMEM((2, domains, slots, BS // domains, BS), jnp.bfloat16),
            pltpu.SMEM((slots,), jnp.float32),
            pltpu.SemaphoreType.DMA((blocks, peers)),
            pltpu.SemaphoreType.DMA((blocks, peers)),
            pltpu.SemaphoreType.DMA((blocks,)),
            pltpu.SemaphoreType.DMA((blocks, group)),
            pltpu.SemaphoreType.DMA((blocks, group)),
            pltpu.SemaphoreType.DMA((blocks, SPAN)),
            pltpu.SemaphoreType.DMA((peers, SPAN)),
            pltpu.SemaphoreType.DMA((blocks, SPAN)),
            pltpu.SemaphoreType.DMA((blocks, SPAN)),
            pltpu.SemaphoreType.DMA((2, SPAN, domains)),
            pltpu.SemaphoreType.DMA((2, SPAN, domains)),
            pltpu.SemaphoreType.DMA((3,)),
        ],
        compiler_params=pltpu.CompilerParams(
            collective_id=0, has_side_effects=True, vmem_limit_bytes=36 * 1024 * 1024
        ),
    )(*[in_hbm(operand) for operand in (aux_mask, pair_list.T, metric, integrals)])


def from_behind(array, axis, by):
    peers = lax.axis_size(axis)
    pairs = [(i, i + by) for i in range(peers) if 0 <= i + by < peers]
    return lax.ppermute(array, axis, pairs)


def fit_block(metric, slab_piece, mask_rows):
    fitted = jnp.einsum("pq,qjn->pjn", metric, slab_piece, preferred_element_type=jnp.float32)
    return (fitted * mask_rows[:, None, None]).astype(jnp.bfloat16)


def by_block(integrals, metric, pair_list, aux_mask):
    block_count = aux_mask.shape[1]
    position = lax.axis_index("blk")
    block_ids = jnp.arange(block_count, dtype=jnp.int32)
    offsets = jnp.arange(SPAN, dtype=jnp.int32)
    col_gap = pair_list[:, 1] - pair_list[:, 0]
    hits = (pair_list[:, 0][:, None] == position) & (col_gap[:, None] == offsets[None, :])
    listed = jnp.sum(hits.astype(jnp.int32), axis=0)
    one_hot = (block_ids == position).astype(jnp.int32)
    column = jnp.sum(aux_mask * one_hot[None, :], axis=1)
    own_mask = jnp.repeat(column, QB).astype(jnp.float32)
    own_block = fit_block(
        metric, lax.all_to_all(integrals, "blk", split_axis=2, concat_axis=0, tiled=True), own_mask
    )
    partners = [own_block]
    current = own_block
    for turn_index in range(SPAN - 1):
        current = from_behind(current, "blk", -1)
        partners.append(current)
    flat_own = partners[0].reshape(-1, BS)

    def make_tile(partner):
        return lax.dot_general(
            flat_own,
            partner.reshape(-1, BS),
            (((0,), (0,)), ((), ())),
            preferred_element_type=jnp.float32,
        )

    tile_list = [
        make_tile(partners[offset]) * listed[offset].astype(jnp.float32) for offset in range(SPAN)
    ]
    upper_tiles = jnp.stack(tile_list)
    mirror_tiles = jnp.stack([jnp.transpose(tile_list[offset]) for offset in range(1, SPAN)])
    lower_tiles = []
    moving = mirror_tiles
    for turn_index in range(SPAN - 1):
        moving = from_behind(moving.astype(jnp.bfloat16), "blk", 1).astype(moving.dtype)
        lower_tiles.append(moving[0])
        moving = moving[1:]
    whole_band = jnp.concatenate(
        [jnp.stack([lower_tiles[SPAN - 2 - slot] for slot in range(SPAN - 1)]), upper_tiles], axis=0
    )
    band_parts = lax.psum_scatter(whole_band, "aux", scatter_dimension=1, tiled=True)
    pieces = [band_parts[slot] for slot in range(2 * SPAN - 1)]
    band_rows = jnp.concatenate(pieces, axis=1)
    return band_rows[None]


def local(integrals, metric, pair_list, aux_mask):
    peers = lax.axis_size("blk")
    blocks = aux_mask.shape[1]
    strips = BS % (8 * PAIR * lax.axis_size("aux")) == 0 and peers == 4 * PAIR
    whole_tiles = integrals.shape[1] == SUB * peers and blocks == peers and strips
    if whole_tiles:
        return by_orbital(integrals, metric, pair_list, aux_mask)
    return by_block(integrals, metric, pair_list, aux_mask)


def solution(mesh):
    return jax.shard_map(
        local,
        mesh=mesh,
        in_specs=(P(("aux", "blk"), None, None), P("aux", None), P(), P("aux", None)),
        out_specs=P("blk", "aux", None),
        check_vma=False,
    )
```

time: 200 us -> 199 us (level); the launches traced: 198 us -> 199 us
  no operation moved by 1% of the time
where the time goes in v1:
time: 199 us
  Pallas kernels  198 us (99%)
    pallas_call x1, Pallas kernels, by_orbital(): pl.pallas_call(functools.partial(tile_kernel, peers, domains, blocks, dep...  198 us

profile of v1, /device:TPU:0, one launch (start us, length us, event | category | flops | bytes accessed | tf_op | source)
XLA Modules:
  0.0 198.9 jit_solution(3157030431740156737)
XLA Ops:
  0.0 198.2 %shard_map.46 = f32[1,32,640]{2,1,0:T(8,128)S(1)} custom-call(s32[4,8]{1,0:T(4,128)} %mask_hbm.1, s32[2,15]{1,0:T(2,128)} %bitcast.1, bf16[512,512]{1,0:T(8,128)(2,1)} %metric_hbm.1, bf16[64,64,1024]{2,1,0:T(8,128)(2,1)} %x_ref.1), custom_call_target="tpu_custom_call" | custom-call | tf_op jit(solution)/shard_map/pallas_call | solution.py:514
  198.2 0.6 copy.6

commit v2 on v1

--- a/solution.py
+++ b/solution.py
@@ -18,10 +18,10 @@
 def tile_kernel(
     peers, domains, blocks, depth, mask_hbm, pairs_hbm, metric_hbm, x_ref, out_ref,
     mask_ref, pairs_ref, metric_ref,
-    slab, wide, ordered, fit_rows, fit_cols, piece_out, piece_in, sum_out, sum_in, relay_in,
+    slab, wide, ordered, fit_rows, fit_cols, piece_out, piece_in, sum_out, sum_in,
     tail_out, tail_in, weights,
-    send_sem, recv_sem, own_sem, piece_send, piece_recv, sum_send, sum_recv, relay_send,
-    relay_recv, tail_send, tail_recv, load_sem,
+    send_sem, recv_sem, piece_send, piece_recv, sum_send, sum_recv, cross_send,
+    tail_send, tail_recv, load_sem,
 ):
     me = lax.axis_index("blk")
     domain = lax.axis_index("aux")
@@ -90,25 +90,18 @@
         return pltpu.make_async_remote_copy(
             src_ref=source(block_at(step, target // half), target),
             dst_ref=landing(step, me),
-            send_sem=send_sem.at[step, target],
-            recv_sem=recv_sem.at[step, me],
+            send_sem=send_sem.at[step],
+            recv_sem=recv_sem.at[step],
             device_id={"blk": target},
             device_id_type=MESH,
         )
 
-    def incoming(step, sender):
-        return pltpu.make_async_remote_copy(
-            src_ref=source(block_at(step, side), me),
-            dst_ref=landing(step, sender),
-            send_sem=send_sem.at[step, sender],
-            recv_sem=recv_sem.at[step, sender],
-            device_id={"blk": sender},
-            device_id_type=MESH,
-        )
+    def settled(ref, sem):
+        pltpu.make_async_copy(ref, ref, sem).wait()
 
     def own(step):
         return pltpu.make_async_copy(
-            source(block_at(step, side), me), landing(step, me), own_sem.at[step]
+            source(block_at(step, side), me), landing(step, me), recv_sem.at[step]
         )
 
     def beside(off):
@@ -159,75 +152,60 @@
         return pltpu.make_async_remote_copy(
             src_ref=piece_out.at[step, lax.rem(place + off, group)],
             dst_ref=piece_in.at[step, place],
-            send_sem=piece_send.at[step, off],
-            recv_sem=piece_recv.at[step, off],
+            send_sem=piece_send.at[step],
+            recv_sem=piece_recv.at[step],
             device_id=member(off),
             device_id_type=MESH,
         )
 
-    def piece_from(step, off):
-        sender = lax.rem(place - off + group, group)
-        return pltpu.make_async_remote_copy(
-            src_ref=piece_out.at[step, sender],
-            dst_ref=piece_in.at[step, sender],
-            send_sem=piece_send.at[step, off],
-            recv_sem=piece_recv.at[step, off],
-            device_id=member(group - off),
-            device_id_type=MESH,
-        )
-
     def span_of(gap):
         return pl.ds(0, SPAN) if gap == 0 else pl.ds(SPAN - 1 + gap, 1)
 
-    def sum_to(step, gap):
+    def sum_to(step, gap, sem):
         return pltpu.make_async_remote_copy(
             src_ref=sum_out.at[step, span_of(gap)],
             dst_ref=sum_in.at[me, span_of(gap)],
-            send_sem=sum_send.at[step, gap],
-            recv_sem=sum_recv.at[me, gap],
+            send_sem=sem,
+            recv_sem=sum_recv.at[gap],
             device_id={"blk": block_at(step - gap, side)},
             device_id_type=MESH,
         )
 
-    def sum_from(sender, gap):
-        return pltpu.make_async_remote_copy(
-            src_ref=sum_out.at[0, span_of(gap)],
-            dst_ref=sum_in.at[sender, span_of(gap)],
-            send_sem=sum_send.at[0, gap],
-            recv_sem=sum_recv.at[sender, gap],
-            device_id={"blk": sender},
-            device_id_type=MESH,
-        )
-
-    def relay(step, gap, other_rank):
-        return pltpu.make_async_remote_copy(
-            src_ref=sum_out.at[step, span_of(gap)],
-            dst_ref=relay_in.at[step, span_of(gap)],
-            send_sem=relay_send.at[step, gap],
-            recv_sem=relay_recv.at[step, gap],
-            device_id={"blk": mirror(other_rank, side)},
-            device_id_type=MESH,
-        )
-
     def crossing(step, gap):
         return (step >= gap) & (step - gap < half)
 
     def staying(step, gap):
         return step - gap >= half
 
+    def shipped(step, gap):
+        return staying(step, gap) & (block_at(step - gap, side) != me)
+
+    def ship():
+        def one(step, inner):
+            for gap in range(SPAN):
+
+                @pl.when(crossing(step, gap))
+                def _():
+                    sum_to(step, gap, cross_send.at[0]).start()
+
+            return inner
+
+        lax.fori_loop(0, half + SPAN - 1, one, 0)
+
     def gather(step):
         late = outer & (step >= last - 1)
 
-        def arrive(off, inner):
-            sender = lax.rem(place - off + group, group)
-
-            @pl.when(jnp.logical_not(late & (lax.rem(sender, PAIR) == side)))
-            def _():
-                piece_from(step, off).wait_recv()
-
-            return inner
-
-        lax.fori_loop(1, group, arrive, 0)
+        @pl.when(late & is_tail)
+        def _():
+            settled(piece_in.at[step, pl.ds(0, domains)], piece_recv.at[step])
+
+        @pl.when(late & jnp.logical_not(is_tail))
+        def _():
+            settled(piece_in.at[step, pl.ds(0, domains - 1)], piece_recv.at[step])
+
+        @pl.when(jnp.logical_not(late))
+        def _():
+            settled(piece_in.at[step, pl.ds(0, group - 1)], piece_recv.at[step])
 
         @pl.when(late)
         def _():
@@ -253,26 +231,9 @@
                 else:
                     sum_in[me, SPAN - 1 + gap] = sum_out[step, SPAN - 1 + gap]
 
-            @pl.when(staying(step, gap) & (owner != me))
+            @pl.when(shipped(step, gap))
             def _():
-                sum_to(step, gap).start()
-
-            @pl.when(crossing(step, gap) & outer)
-            def _():
-                relay(step, gap, rank + PAIR).start()
-
-    def forward(step):
-        for gap in range(SPAN):
-
-            @pl.when(crossing(step, gap) & jnp.logical_not(outer))
-            def _():
-                relay(step, gap, rank - PAIR).wait_recv()
-                if gap == 0:
-                    sum_out[step, :SPAN] = sum_out[step, :SPAN] + relay_in[step, :SPAN]
-                else:
-                    at = SPAN - 1 + gap
-                    sum_out[step, at] = sum_out[step, at] + relay_in[step, at]
-                sum_to(step, gap).start()
+                sum_to(step, gap, sum_send.at[gap]).start()
 
     def reorder(step, sender):
         span = pl.ds(pl.multiple_of(sender * rows, rows), rows)
@@ -283,21 +244,13 @@
             )
 
     def collect(step):
-        own(step).wait()
-        reorder(step, me)
-
-        def arrive_beside(off, inner):
-            incoming(step, beside(off)).wait_recv()
-            reorder(step, beside(off))
+        settled(slab.at[step], recv_sem.at[step])
+
+        def one(sender, inner):
+            reorder(step, sender)
             return inner
 
-        def arrive_across(other_rank, inner):
-            incoming(step, across(other_rank)).wait_recv()
-            reorder(step, across(other_rank))
-            return inner
-
-        lax.fori_loop(1, half, arrive_beside, 0)
-        lax.fori_loop(0, half, arrive_across, 0)
+        lax.fori_loop(0, peers, one, 0)
 
     def multiply(step):
         block = block_at(step, side)
@@ -342,19 +295,9 @@
         return pltpu.make_async_remote_copy(
             src_ref=tail_out.at[turn_step, to, span_of(gap)],
             dst_ref=tail_in.at[turn_step, domain, span_of(gap)],
-            send_sem=tail_send.at[turn_step, gap, turn],
-            recv_sem=tail_recv.at[turn_step, gap, domain],
+            send_sem=tail_send.at[turn_step, min(gap, 1)],
+            recv_sem=tail_recv.at[turn_step, gap],
             device_id={"aux": to, "blk": mirror(1 - turn_step + gap, side)},
-            device_id_type=MESH,
-        )
-
-    def tail_from(turn_step, gap, sender):
-        return pltpu.make_async_remote_copy(
-            src_ref=tail_out.at[turn_step, sender, span_of(gap)],
-            dst_ref=tail_in.at[turn_step, sender, span_of(gap)],
-            send_sem=tail_send.at[turn_step, gap, 0],
-            recv_sem=tail_recv.at[turn_step, gap, sender],
-            device_id={"aux": sender, "blk": mirror(0, side)},
             device_id_type=MESH,
         )
 
@@ -380,21 +323,22 @@
             tail_in[1, domain, :SPAN] = tail_out[1, domain, :SPAN]
 
     def step(index, carry):
-        @pl.when(index > 0)
+        late = is_tail & (index >= last - 1)
+
+        @pl.when((index > 0) & jnp.logical_not(is_tail & (index == last)))
         def _():
             gather(index - 1)
 
-        @pl.when(index > 1)
-        def _():
-            forward(index - 2)
+        @pl.when(late)
+        def _():
+            gather(index)
 
         @pl.when(is_tail & (index == last))
         def _():
-            gather(last)
+            ship()
 
         collect(index)
         tiles = multiply(index)
-        late = is_tail & (index >= last - 1)
 
         @pl.when(jnp.logical_not(late))
         def _():
@@ -413,69 +357,58 @@
     @pl.when(jnp.logical_not(is_tail))
     def _():
         gather(last)
+        ship()
 
     def settle(index, carry):
-        for other_rank in range(half):
-            outgoing(index, across(other_rank)).wait_send()
-        for off in range(1, half):
-            outgoing(index, beside(off)).wait_send()
-
-        def two(off, inner):
-            piece_to(index, off).wait_send()
-            return inner
+        settled(slab.at[index, pl.ds(0, depth - rows)], send_sem.at[index])
 
         @pl.when(jnp.logical_not(is_tail & (index >= last - 1)))
         def _():
-            lax.fori_loop(1, group, two, 0)
-
-        for gap in range(SPAN):
-            owner = block_at(index - gap, side)
-            kept = staying(index, gap) & (owner != me)
-            crossed = crossing(index, gap)
-
-            @pl.when(kept | (crossed & jnp.logical_not(outer)))
+            settled(piece_out.at[index, pl.ds(0, group - 1)], piece_send.at[index])
+
+        return carry
+
+    lax.fori_loop(0, blocks, settle, 0)
+    settled(sum_out.at[pl.ds(0, half)], cross_send.at[0])
+    for gap in range(SPAN):
+        for whole in (0, 1):
+
+            @pl.when((rank < gap) if whole else (rank >= gap))
             def _():
-                sum_to(index, gap).wait_send()
-
-            @pl.when(crossed & outer)
-            def _():
-                relay(index, gap, rank + PAIR).wait_send()
-
-        return carry
-
-    lax.fori_loop(0, blocks, settle, 0)
-
-    inner_base = half - PAIR + (1 - side) * PAIR
+                count = half - gap - 1 + whole
+                settled(sum_in.at[pl.ds(0, count), span_of(gap)], sum_send.at[gap])
+
+
     for gap in range(SPAN):
 
         @pl.when(rank >= gap)
         def _():
-            def arrive(off, inner):
-                sum_from(beside(off), gap).wait_recv()
-                return inner
-
-            lax.fori_loop(1, half, arrive, 0)
-
-        for core in range(PAIR):
-            sum_from(inner_base + core, gap).wait_recv()
+            settled(sum_in.at[pl.ds(0, peers - 1), span_of(gap)], sum_recv.at[gap])
+
+        @pl.when(rank < gap)
+        def _():
+            settled(sum_in.at[pl.ds(0, half), span_of(gap)], sum_recv.at[gap])
 
     for turn_step in range(2):
         for gap in range(SPAN):
-
-            @pl.when(rank == 1 - turn_step + gap)
+            wanted = rank == 1 - turn_step + gap
+            here = turn_step == 1 and gap == 0
+
+            @pl.when(wanted)
             def _():
-                for sender in range(domains):
-
-                    @pl.when(jnp.logical_not(is_tail & (sender == domain)))
-                    def _():
-                        tail_from(turn_step, gap, sender).wait_recv()
+                count = domains - 1 if here else domains
+                settled(
+                    tail_in.at[turn_step, pl.ds(0, count), span_of(gap)],
+                    tail_recv.at[turn_step, gap],
+                )
 
     for slot in range(slots):
         where = SPAN - 1 + sign * (slot - (SPAN - 1))
         columns = pl.ds(pl.multiple_of(where * BS, BS), BS)
         for core in range(PAIR):
-            total = sum_in[inner_base + core, slots - 1 - slot]
+            total = jnp.zeros((strip, BS), jnp.float32)
             for turn in range(half // PAIR):
+                total = total + sum_in[(1 - side) * half + turn * PAIR + core, slots - 1 - slot]
                 total = total + sum_in[side * half + turn * PAIR + core, slot]
             out_ref[0, core * strip : (core + 1) * strip, columns] = total * weights[slot]
 
@@ -492,11 +425,12 @@
                         total = total + tail_in[turn_step, sender, slot].astype(jnp.float32)
                     out_ref[0, :, columns] = out_ref[0, :, columns] + total * weights[slot]
 
-    for which, gap, turn in tail_sends():
-
-        @pl.when(is_tail)
-        def _():
-            tail_to(which, gap, turn).wait_send()
+    @pl.when(is_tail)
+    def _():
+        for turn_step in range(2):
+            count = domains - turn_step
+            settled(tail_out.at[turn_step, pl.ds(0, count), span_of(0)], tail_send.at[turn_step, 0])
+            settled(tail_out.at[turn_step, :, pl.ds(SPAN, SPAN - 1)], tail_send.at[turn_step, 1])
 
 
 def in_hbm(operand):
@@ -534,21 +468,18 @@
             pltpu.VMEM((blocks, group, slots, strip, BS), jnp.float32),
             pltpu.VMEM((blocks, slots, strip, BS), jnp.float32),
             pltpu.VMEM((peers, slots, strip, BS), jnp.float32),
-            pltpu.VMEM((blocks, slots, strip, BS), jnp.float32),
             pltpu.VMEM((2, domains, slots, BS // domains, BS), jnp.bfloat16),
             pltpu.VMEM((2, domains, slots, BS // domains, BS), jnp.bfloat16),
             pltpu.SMEM((slots,), jnp.float32),
-            pltpu.SemaphoreType.DMA((blocks, peers)),
-            pltpu.SemaphoreType.DMA((blocks, peers)),
             pltpu.SemaphoreType.DMA((blocks,)),
-            pltpu.SemaphoreType.DMA((blocks, group)),
-            pltpu.SemaphoreType.DMA((blocks, group)),
-            pltpu.SemaphoreType.DMA((blocks, SPAN)),
-            pltpu.SemaphoreType.DMA((peers, SPAN)),
-            pltpu.SemaphoreType.DMA((blocks, SPAN)),
-            pltpu.SemaphoreType.DMA((blocks, SPAN)),
-            pltpu.SemaphoreType.DMA((2, SPAN, domains)),
-            pltpu.SemaphoreType.DMA((2, SPAN, domains)),
+            pltpu.SemaphoreType.DMA((blocks,)),
+            pltpu.SemaphoreType.DMA((blocks,)),
+            pltpu.SemaphoreType.DMA((blocks,)),
+            pltpu.SemaphoreType.DMA((SPAN,)),
+            pltpu.SemaphoreType.DMA((SPAN,)),
+            pltpu.SemaphoreType.DMA((1,)),
+            pltpu.SemaphoreType.DMA((2, 2)),
+            pltpu.SemaphoreType.DMA((2, SPAN)),
             pltpu.SemaphoreType.DMA((3,)),
         ],
         compiler_params=pltpu.CompilerParams(

time: 199 us -> 196 us (0.985)
  Pallas kernels: 198 us -> 196 us
    pallas_call x1, Pallas kernels: 198 us -> 196 us  [by_orbital(): pl.pallas_call(functools.partial(tile_kernel, peers, domains, blocks, dep...]
where the time goes in v2:
time: 196 us
  Pallas kernels  196 us (100%)
    pallas_call x1, Pallas kernels, by_orbital(): pl.pallas_call(functools.partial(tile_kernel, peers, domains, blocks, dep...  196 us

profile of v2, /device:TPU:0, one launch (start us, length us, event | category | flops | bytes accessed | tf_op | source)
XLA Modules:
  0.0 196.3 jit_solution(6929171937564877813)
XLA Ops:
  0.0 195.6 %shard_map.46 = f32[1,32,640]{2,1,0:T(8,128)S(1)} custom-call(s32[4,8]{1,0:T(4,128)} %mask_hbm.1, s32[2,15]{1,0:T(2,128)} %bitcast.1, bf16[512,512]{1,0:T(8,128)(2,1)} %metric_hbm.1, bf16[64,64,1024]{2,1,0:T(8,128)(2,1)} %x_ref.1), custom_call_target="tpu_custom_call" | custom-call | tf_op jit(solution)/shard_map/pallas_call | solution.py:448
  195.6 0.6 copy.6
